TPU v7x, 256 devices: a whole 4x4x8 slice. The times are simulated.
256 devices in a mesh: dp: 8 (over x, y_lo), tensor: 32 (over z, y_hi, core).
Axes of the slice: x: 4, y: 4 (y_hi: 2, y_lo: 2; y = y_hi * 2 + y_lo), z: 8, core: 2. Of those that a mesh axis runs over, the one named last changes fastest.
Arguments:
- real_feats: bfloat16 [16384, 1536], P(('dp', 'tensor')), may hold values from -6 to 6
- fake_feats: bfloat16 [16384, 1536], P(('dp', 'tensor')), may hold values from -6 to 6
- mix_num: int32 [16384], P(('dp', 'tensor')), may hold values from 0 to 256
- w_first: bfloat16 [1536, 12288], P(None, 'tensor'), may hold values from -0.15625 to 0.15625
- bias: float32 [12288], P('tensor'), may hold values from -3 to 3
- head: float32 [12288], P('tensor'), may hold values from -0.0546875 to 0.0546875
Outputs:
- grad_w: float32 [1536, 12288], P('dp', 'tensor')
- grad_bias: float32 [12288], P('tensor')
- grad_head: float32 [12288], P('tensor')
- penalty: float32 [], replicated
All inputs are finite; a program needn't handle non-finite values.
Results may differ from a plain program's by a relative error of at most 0.0005.
Values may be sent and summed in bfloat16 or wider, within the bound.
No kernel may reach another device: no remote copies, remote signals or barrier semaphores. Data moves between devices by JAX's collectives and lax.ppermute only.
A program may use at most 64 MiB of HBM per device.

v0:
```python
import jax
import jax.numpy as jnp
from jax import lax
from jax.sharding import Mesh
from jax.sharding import PartitionSpec as P

TENSOR = ("tensor_0", "tensor_1", "tensor_2")
DP_TENSOR = ("dp", "tensor_0", "tensor_1", "tensor_2")


def sent_to_all(array, axis):
    copies = jnp.broadcast_to(array, (lax.axis_size(axis), *array.shape))
    return lax.all_to_all(copies, axis, split_axis=0, concat_axis=0, tiled=True)


def over_copies(array, axis):
    everything = sent_to_all(array, axis)
    return jnp.sum(everything, axis=0)


def in_order(tiles, dim):
    lengths = list(tiles.shape[1:])
    lengths[dim] *= tiles.shape[0]
    return jnp.moveaxis(tiles, 0, dim).reshape(lengths)


def gather_in_order(array, axes, order):
    tiles = array
    for k in order:
        tiles = lax.all_gather(tiles, axes[k])
    done = order[::-1]
    back = [done.index(k) for k in range(len(axes))]
    tiles = tiles.transpose(*back, *range(len(axes), tiles.ndim))
    return tiles.reshape(-1, *array.shape)


def whole_of(array, axes, order, dim):
    return in_order(gather_in_order(array, axes, order), dim)


def cut_along(array, dim, length):
    lengths = array.shape
    tiles = array.reshape(*lengths[:dim], length, lengths[dim] // length, *lengths[dim + 1 :])
    return jnp.moveaxis(tiles, dim, 0)


def sum_at_owner(array, axis, dim):
    length = lax.axis_size(axis)
    tiles = lax.all_to_all(cut_along(array, dim, length), axis, 0, 0, tiled=True)
    return jnp.sum(tiles, axis=0)


def packed_total(arrays, axis):
    ravelled, at, finished = (jnp.concatenate([a.reshape(-1) for a in arrays]), 0, [])
    running = over_copies(ravelled, axis)
    for a in arrays:
        finished.append(running[at : at + a.size].reshape(a.shape))
        at += a.size
    return tuple(finished)


def row_contract(left, right):
    return lax.dot_general(
        left, right, (((0,), (0,)), ((), ())), preferred_element_type=jnp.float32
    )


def local(real_feats, fake_feats, mix_num, w_first, bias, head):
    coef = mix_num.astype(jnp.float32) / 256.0
    real_f = real_feats.astype(jnp.float32)
    mixed = (real_f + coef[:, None] * (fake_feats.astype(jnp.float32) - real_f)).astype(
        jnp.bfloat16
    )
    group = lax.all_gather(mixed, TENSOR, axis=0, tiled=True)
    z = jnp.dot(group, w_first, preferred_element_type=jnp.float32) + bias
    sg = jax.nn.sigmoid(z)
    d1 = sg * (1.0 + z * (1.0 - sg))
    d2 = sg * (1.0 - sg) * (2.0 + z * (1.0 - 2.0 * sg))
    u = (d1 * head).astype(jnp.bfloat16)
    total_rows = group.shape[0] * lax.axis_size("dp")
    whole = lax.dot_general(
        u, w_first, (((1,), (1,)), ((), ())), preferred_element_type=jnp.float32
    )
    grad_cols = lax.psum_scatter(
        whole.astype(jnp.bfloat16), TENSOR, scatter_dimension=1, tiled=True
    ).astype(jnp.float32)
    squares = over_copies(jnp.sum(grad_cols * grad_cols, axis=1), TENSOR)
    norm = jnp.sqrt(squares + 1e-06)
    scale = 20.0 * (norm - 1.0) / norm
    scaled_cols = (scale[:, None] * grad_cols).astype(jnp.bfloat16)
    loss = over_copies(jnp.sum((norm - 1.0) ** 2), "dp")
    big = whole_of(scaled_cols, TENSOR, (1, 0, 2), 1)
    penalty = 10.0 * loss / total_rows
    p = jnp.dot(big, w_first, preferred_element_type=jnp.float32)
    dz = p * head * d2
    dzb = dz.astype(jnp.bfloat16)
    partial_w = row_contract(group, dzb)
    partial_w = partial_w + row_contract(big, u)
    grad_w = sum_at_owner(partial_w, "dp", 0)
    grad_bias, grad_head = packed_total((jnp.sum(dz, axis=0), jnp.sum(p * d1, axis=0)), "dp")
    return (grad_w, grad_bias, grad_head, penalty)


def solution(mesh):
    torus = Mesh(
        mesh.devices.reshape(mesh.shape["dp"], 8, 2, 2), ("dp", "tensor_0", "tensor_1", "tensor_2")
    )
    return jax.shard_map(
        local,
        mesh=torus,
        in_specs=(
            P(DP_TENSOR, None),
            P(DP_TENSOR, None),
            P(DP_TENSOR),
            P(None, TENSOR),
            P(TENSOR),
            P(TENSOR),
        ),
        out_specs=(P("dp", TENSOR), P(TENSOR), P(TENSOR), P()),
        check_vma=False,
    )
```

profile of v0, /device:TPU:1, one launch (start us, length us, event | category | flops | bytes accessed | tf_op | source)
XLA Modules:
  0.0 429.0 jit_solution(8761464536619151029)
XLA Ops:
  7.2 0.0 copy-start
  7.2 0.0 all-gather.7.cloned.1.call-start
  7.2 0.7 convert_multiply_fusion.2
  8.0 1.8 fusion.7
  9.8 0.0 all-gather.7.cloned.1.call-update
  9.8 0.0 copy-start.3
  9.8 0.0 copy-start.4
  9.8 0.0 reduce-scatter.2.cloned.1.call-start
  9.9 99.4 %all-gather.7.cloned.1.call-done = bf16[2048,1536]{1,0:T(8,128)(2,1)} async-done(((bf16[64,1536]{1,0:T(8,128)(2,1)}), bf16[2048,1536]{1,0:T(8,128)(2,1)}) %all-gather.7.cloned.1.call-update) | async-done | bytes 6291472 | tf_op jit(solution)/shard_map/all_gather | solution.py:74
  109.3 5.5 %fusion.15 = f32[2048,384]{1,0:T(8,128)S(1)} fusion(bf16[2048,1536]{1,0:T(8,128)(2,1)} %all-gather.7.cloned.1.call-done, bf16[1536,384]{1,0:T(8,128)(2,1)S(1)} %copy-done), kind=kOutput, calls=%fused_computation.29 | convolution fusion | flops 2415919104 | bytes 10616832 | tf_op jit(solution)/shard_map/dot_general | solution.py:75
  114.7 1.6 copy-done.5
  116.4 0.0 copy-done.4
  116.4 5.7 %convolution_convert_fusion = bf16[2048,1536]{0,1:T(8,128)(2,1)} fusion(bf16[1536,384]{1,0:T(8,128)(2,1)S(1)} %copy-done, f32[384]{0:T(512)S(1)} %copy-done.4, f32[2048,384]{1,0:T(8,128)S(1)} %fusion.15, f32[384]{0:T(512)S(1)} %copy-done.3), kind=kOutput, calls=%fused_computation | convolution fusion | flops 2426929152 | bytes 10619904 | tf_op jit(solution)/shard_map/dot_general | solution.py:81
  122.1 0.0 reduce-scatter.2.cloned.1.call-update
  122.1 0.0 all-gather.9.cloned.1.call-start
  122.1 129.7 %reduce-scatter.2.cloned.1.call-done = bf16[2048,48]{0,1:T(8,128)(2,1)} async-done(((bf16[2048,1536]{0,1:T(8,128)(2,1)}), bf16[2048,48]{0,1:T(8,128)(2,1)}) %reduce-scatter.2.cloned.1.call-update) | async-done | bytes 196624 | tf_op jit(solution)/shard_map/reduce_scatter | solution.py:84
  251.9 1.0 fusion.8
  252.9 0.1 broadcast_in_dim.6
  253.0 23.0 %all_to_all.23 = f32[32,1,2048]{2,1,0:T(1,128)S(1)} all-to-all(f32[32,1,2048]{2,1,0:T(1,128)S(1)} %broadcast_in_dim.6), channel_id=1, replica_groups=mesh['dp'=8,'tensor_0'=8,'tensor_1'=2,'tensor_2'=2] {'tensor_0','tensor_..., dimensions={0} | all-to-all | bytes 524288 | tf_op jit(solution)/shard_map/all_to_all | solution.py:13
  276.0 0.2 reduce_sum.73
  276.2 0.6 multiply_reduce_fusion.1
  276.8 1.0 fusion.9
  277.8 8.2 %all-gather = bf16[4096,48]{0,1:T(8,128)(2,1)S(1)} all-gather(bf16[2048,48]{0,1:T(8,128)(2,1)S(1)} %fusion.9), channel_id=2, replica_groups=mesh['dp'=8,'tensor_0'=8,'tensor_1'=2,'tensor_2'=2] {'tensor_1'}, dimensions={0}, use_global_device_ids=true | all-gather | bytes 589824 | tf_op jit(solution)/shard_map/all_gather | solution.py:30
  286.0 0.8 copy.28
  286.8 0.0 all-gather.9.cloned.1.call-update
  286.8 0.0 all-gather.11.cloned.1.call-start
  286.8 41.3 %all-gather.9.cloned.1.call-done = bf16[16,2048,48]{1,2,0:T(8,128)(2,1)} async-done(((bf16[2,2048,48]{1,2,0:T(8,128)(2,1)}), bf16[16,2048,48]{1,2,0:T(8,128)(2,1)}) %all-gather.9.cloned.1.call-update) | async-done | bytes 3145744 | tf_op jit(solution)/shard_map/all_gather | solution.py:30
  328.1 0.0 all-gather.11.cloned.1.call-update
  328.1 1.2 broadcast_in_dim.16
  329.4 4.9 %all-to-all-start.3 = ((f32[8,1,1]{2,1,0:T(1,128)}), f32[8,1,1]{2,1,0:T(1,128)S(1)}, u32[]{:S(2)}, u32[]{:S(2)}) async-start(f32[8,1,1]{2,1,0:T(1,128)} %broadcast_in_dim.16), calls=%async_computation.4 | async-start | bytes 8192 | tf_op jit(solution)/shard_map/all_to_all | solution.py:13
  334.3 17.5 %all-gather.11.cloned.1.call-done = bf16[16,2,2048,48]{2,3,1,0:T(8,128)(2,1)} async-done(((bf16[8,2,2048,48]{2,3,1,0:T(8,128)(2,1)}), bf16[16,2,2048,48]{2,3,1,0:T(8,128)(2,1)}) %all-gather.11.cloned.1.call-update) | async-done | bytes 6291472 | tf_op jit(solution)/shard_map/all_gather | solution.py:30
  351.8 3.5 copy.18
  355.3 0.0 copy-start.1
  355.3 0.1 copy-done.6
  355.5 5.4 %fusion.12 = (f32[384]{0:T(512)S(1)}, bf16[2048,384]{1,0:T(8,128)(2,1)S(1)}, f32[384]{0:T(512)S(1)}) fusion(f32[2048,384]{1,0:T(8,128)S(1)} %copy-done.6, f32[384]{0:T(512)S(1)} %copy-done.3, f32[384]{0:T(512)S(1)} %copy-done.4, bf16[2048,1536]{0,1:T(8,128)(2,1)S(1)} %bitcast.22, bf16[1536,384]{1,0:T(8,128)(2,1)S(1)} %copy-done), kind=kOutput, calls=%fused_computation.27 | convolution fusion | flops 2431646720 | bytes 12195840 | tf_op jit(solution)/shard_map/dot_general | solution.py:94
  361.0 4.9 %fusion.4 = f32[1536,384]{1,0:T(8,128)} fusion(bf16[2048,1536]{1,0:T(8,128)(2,1)S(1)} %bitcast.30, bf16[2048,384]{1,0:T(8,128)(2,1)S(1)} %get-tuple-element.5), kind=kOutput, calls=%fused_computation.11 | convolution fusion | flops 2415919104 | bytes 10223616 | tf_op jit(solution)/shard_map/dot_general | solution.py:63
  365.8 0.0 all-to-all-done.3
  365.8 0.6 broadcast_in_dim.7
  366.5 4.6 %all-to-all-start.2 = ((f32[8,1,768]{2,1,0:T(1,128)}), f32[8,1,768]{2,1,0:T(1,128)S(1)}, u32[]{:S(2)}, u32[]{:S(2)}) async-start(f32[8,1,768]{2,1,0:T(1,128)} %broadcast_in_dim.7), calls=%async_computation.3 | async-start | bytes 49152 | tf_op jit(solution)/shard_map/all_to_all | solution.py:13
  371.1 9.4 %convolution_add_fusion = f32[1536,384]{1,0:T(8,128)} fusion(f32[1536,384]{1,0:T(8,128)} %fusion.4, bf16[2048,1536]{0,1:T(8,128)(2,1)} %bitcast.23, f32[384]{0:T(512)S(1)} %copy-done.4, f32[2048,384]{1,0:T(8,128)} %copy-done.5, f32[384]{0:T(512)S(1)} %copy-done.3), kind=kOutput, calls=%fused_computation.10 | convolution fusion | flops 2424373248 | bytes 14158848 | tf_op jit(solution)/shard_map/dot_general | solution.py:63
  380.5 0.0 all-to-all-done.2
  380.5 0.6 copy-done.2
  381.1 5.1 %all-to-all-start.1 = ((f32[8,192,384]{2,1,0:T(8,128)}), f32[8,192,384]{2,1,0:T(8,128)S(1)}, u32[]{:S(2)}, u32[]{:S(2)}) async-start(f32[8,192,384]{2,1,0:T(8,128)} %bitcast.26), calls=%async_computation.2 | async-start | bytes 4718592 | tf_op jit(solution)/shard_map/all_to_all | solution.py:49
  386.3 0.6 reduce_sum.79
  387.5 0.8 reduce_sum.77
  388.3 0.6 fusion.14
  388.9 31.6 %all-to-all-done.1 = f32[8,192,384]{2,1,0:T(8,128)S(1)} async-done(((f32[8,192,384]{2,1,0:T(8,128)}), f32[8,192,384]{2,1,0:T(8,128)S(1)}, u32[]{:S(2)}, u32[]{:S(2)}) %all-to-all-start.1) | async-done | bytes 2359328 | tf_op jit(solution)/shard_map/all_to_all | solution.py:49
  420.5 0.8 reduce_sum.74
  (12 shorter events, 0.0 us)
Async XLA Ops:
  7.2 102.1 %copy-start = (bf16[1536,384]{1,0:T(8,128)(2,1)S(1)}, bf16[1536,384]{1,0:T(8,128)(2,1)}, u32[]{:S(2)}) copy-start(bf16[1536,384]{1,0:T(8,128)(2,1)} %param.9) | copy-start | bytes 3538948
  7.2 102.1 %all-gather.7.cloned.1.call-start = ((), (), s32[]{:S(2)}) async-start(), calls=%async_computation.5 | async-start | bytes 6488064 | tf_op jit(solution)/shard_map/all_gather | solution.py:74
  9.8 106.6 %copy-start.3 = (f32[384]{0:T(512)S(1)}, f32[384]{0:T(512)}, u32[]{:S(2)}) copy-start(f32[384]{0:T(512)} %param.10) | copy-start | bytes 4612
  9.8 106.6 %copy-start.4 = (f32[384]{0:T(512)S(1)}, f32[384]{0:T(512)}, u32[]{:S(2)}) copy-start(f32[384]{0:T(512)} %param.11) | copy-start | bytes 4612
  9.8 242.0 %reduce-scatter.2.cloned.1.call-start = ((), (), s32[]{:S(2)}) async-start(), calls=%async_computation.6 | async-start | bytes 6488064 | tf_op jit(solution)/shard_map/reduce_scatter | solution.py:84
  114.7 1.6 copy-start.5
  122.1 206.0 %all-gather.9.cloned.1.call-start = ((), (), s32[]{:S(2)}) async-start(), calls=%async_computation.7 | async-start | bytes 3538944 | tf_op jit(solution)/shard_map/all_gather | solution.py:30
  286.8 65.0 %all-gather.11.cloned.1.call-start = ((), (), s32[]{:S(2)}) async-start(), calls=%async_computation.8 | async-start | bytes 9437184 | tf_op jit(solution)/shard_map/all_gather | solution.py:30
  329.4 36.5 %all-to-all-start.3 = ((f32[8,1,1]{2,1,0:T(1,128)}), f32[8,1,1]{2,1,0:T(1,128)S(1)}, u32[]{:S(2)}, u32[]{:S(2)}) async-start(f32[8,1,1]{2,1,0:T(1,128)} %broadcast_in_dim.16), calls=%async_computation.4 | async-start | bytes 8192 | tf_op jit(solution)/shard_map/all_to_all | solution.py:13
  351.8 3.7 copy-start.6
  351.8 9.2 %slice-start = ((s8[6291456]{0:T(1024)(128)(4,1)}), s8[4194304]{0:T(1024)(128)(4,1)S(1)}, s32[]{:S(2)}) async-start(s8[6291456]{0:T(1024)(128)(4,1)} %bitcast.29), calls=%async_computation.9 | async-start | bytes 8388608
  355.3 5.6 %copy-start.1 = (bf16[8,2,2,2048,48]{3,4,2,1,0:T(8,128)(2,1)}, bf16[8,2,2,2048,48]{3,4,2,1,0:T(8,128)(2,1)S(1)}, u32[]{:S(2)}) copy-start(bf16[8,2,2,2048,48]{3,4,2,1,0:T(8,128)(2,1)S(1)} %copy.18) | copy-start | bytes 18874372
  355.5 5.5 %slice-start.1 = ((s8[6291456]{0:T(1024)(128)(4,1)}), s8[2097152]{0:T(1024)(128)(4,1)S(1)}, s32[]{:S(2)}) async-start(s8[6291456]{0:T(1024)(128)(4,1)} %bitcast.29), calls=%async_computation.10 | async-start | bytes 4194304
  366.5 14.0 %all-to-all-start.2 = ((f32[8,1,768]{2,1,0:T(1,128)}), f32[8,1,768]{2,1,0:T(1,128)S(1)}, u32[]{:S(2)}, u32[]{:S(2)}) async-start(f32[8,1,768]{2,1,0:T(1,128)} %broadcast_in_dim.7), calls=%async_computation.3 | async-start | bytes 49152 | tf_op jit(solution)/shard_map/all_to_all | solution.py:13
  380.5 0.6 copy-start.2
  381.1 39.4 %all-to-all-start.1 = ((f32[8,192,384]{2,1,0:T(8,128)}), f32[8,192,384]{2,1,0:T(8,128)S(1)}, u32[]{:S(2)}, u32[]{:S(2)}) async-start(f32[8,192,384]{2,1,0:T(8,128)} %bitcast.26), calls=%async_computation.2 | async-start | bytes 4718592 | tf_op jit(solution)/shard_map/all_to_all | solution.py:49
Sparse Core Ops, SparseCore 0:
  11.3 97.8 all-gather.6
  122.2 129.6 reduce-scatter.1
  286.9 41.1 all-gather.8
  329.7 21.9 all-gather.10
where the time goes:
time: 429 us
  waiting for transfers between devices  320 us (75%)
  blocking collectives  31.2 us (7%)
  matrix products  30.9 us (7%)
  between operations  15.7 us (4%)
  starting transfers between devices  14.8 us (3%)
  local copies, waits for them, and re-layouts  9.31 us (2%)
  other arithmetic  7.51 us (2%)
    reduce_scatter x1, waiting for transfers between devices, local(): lax.psum_scatter(whole.astype(jnp.bfloat16), TENSOR, scatter_dimension=1,...  130 us
    all_gather x1, waiting for transfers between devices, local(): group = lax.all_gather(mixed, TENSOR, axis=0, tiled=True)  99.4 us
    all_gather x2, waiting for transfers between devices, gather_in_order(): tiles = lax.all_gather(tiles, axes[k])  58.8 us
    all_to_all x1, waiting for transfers between devices, sum_at_owner(): lax.all_to_all(cut_along(array, dim, length), axis, 0, 0, tiled=True)  31.6 us
    all_to_all x1, blocking collectives, sent_to_all(): return lax.all_to_all(copies, axis, split_axis=0, concat_axis=0, tiled=True)  23 us
    dot_general x2, matrix products, row_contract(): lax.dot_general(left, right, (((0,), (0,)), ((), ())), preferred_element_...  14.3 us
    all_to_all x2, starting transfers between devices, sent_to_all(): return lax.all_to_all(copies, axis, split_axis=0, concat_axis=0, tiled=True)  9.52 us
  transfers between devices with their start and end apart: 7, of which 5 were waited for; matrix products, arithmetic and copies ran while one was open for 6% of the time, Pallas kernels for 0%

commit v1 on v0

--- a/solution.py
+++ b/solution.py
@@ -71,7 +71,8 @@
     mixed = (real_f + coef[:, None] * (fake_feats.astype(jnp.float32) - real_f)).astype(
         jnp.bfloat16
     )
-    group = lax.all_gather(mixed, TENSOR, axis=0, tiled=True)
+    repeated = jnp.stack([mixed] * lax.axis_size(TENSOR))
+    group = jnp.concatenate(lax.all_to_all(repeated, TENSOR, 0, 0), axis=0)
     z = jnp.dot(group, w_first, preferred_element_type=jnp.float32) + bias
     sg = jax.nn.sigmoid(z)
     d1 = sg * (1.0 + z * (1.0 - sg))

time: 429 us -> 484 us (1.13)
  blocking collectives: 31.2 us -> 184 us
  waiting for transfers between devices: 320 us -> 221 us
    all_to_all x0 -> x1, blocking collectives: none -> 153 us  [local(): group = jnp.concatenate(lax.all_to_all(repeated, TENSOR, 0, 0), axis=0)]
    all_gather x1 -> x0, waiting for transfers between devices: 99.4 us -> none  [local(): group = lax.all_gather(mixed, TENSOR, axis=0, tiled=True)]
  transfers between devices with their start and end apart: 7 -> 6, of which waited for: 5 -> 4; matrix products, arithmetic and copies ran while one was open for 6% -> 5% of each run, Pallas kernels for 0% -> 0%
where the time goes in v1:
time: 484 us
  waiting for transfers between devices  221 us (46%)
  blocking collectives  184 us (38%)
  matrix products  28.8 us (6%)
  between operations  15.6 us (3%)
  starting transfers between devices  14.8 us (3%)
  local copies, waits for them, and re-layouts  12.7 us (3%)
  other arithmetic  6.83 us (1%)
    all_to_all x1, blocking collectives, local(): group = jnp.concatenate(lax.all_to_all(repeated, TENSOR, 0, 0), axis=0)  153 us
    reduce_scatter x1, waiting for transfers between devices, local(): lax.psum_scatter(whole.astype(jnp.bfloat16), TENSOR, scatter_dimension=1,...  130 us
    all_gather x2, waiting for transfers between devices, gather_in_order(): tiles = lax.all_gather(tiles, axes[k])  58.9 us
    all_to_all x1, waiting for transfers between devices, sum_at_owner(): lax.all_to_all(cut_along(array, dim, length), axis, 0, 0, tiled=True)  31.6 us
    all_to_all x1, blocking collectives, sent_to_all(): return lax.all_to_all(copies, axis, split_axis=0, concat_axis=0, tiled=True)  23 us
    dot_general x2, matrix products, row_contract(): lax.dot_general(left, right, (((0,), (0,)), ((), ())), preferred_element_...  14.3 us
  transfers between devices with their start and end apart: 6, of which 4 were waited for; matrix products, arithmetic and copies ran while one was open for 5% of the time, Pallas kernels for 0%

profile of v1, /device:TPU:1, one launch (start us, length us, event | category | flops | bytes accessed | tf_op | source)
XLA Modules:
  0.0 483.9 jit_solution(15541710794639571504)
XLA Ops:
  7.2 0.0 copy-start
  7.2 0.0 reduce-scatter.2.cloned.1.call-start
  7.2 0.7 convert_multiply_fusion.2
  8.0 1.1 fusion.7
  9.1 0.7 stack.2
  9.8 153.0 %all_to_all.28 = bf16[32,64,1536]{2,1,0:T(8,128)(2,1)S(1)} all-to-all(bf16[32,64,1536]{2,1,0:T(8,128)(2,1)S(1)} %stack.2), channel_id=1, replica_groups=mesh['dp'=8,'tensor_0'=8,'tensor_1'=2,'tensor_2'=2] {'tensor_0','tensor_..., dimensions={0} | all-to-all | bytes 12582912 | tf_op jit(solution)/shard_map/all_to_all | solution.py:75
  162.8 2.6 copy-done.1
  165.4 0.0 copy-done
  165.4 3.4 fusion.15
  168.9 0.0 copy-start.6
  168.9 1.6 copy-done.6
  170.5 0.0 copy-done.4
  170.5 5.7 %convolution_convert_fusion = bf16[2048,1536]{0,1:T(8,128)(2,1)} fusion(bf16[1536,384]{1,0:T(8,128)(2,1)S(1)} %copy-done, f32[384]{0:T(512)S(1)} %copy-done.5, f32[2048,384]{1,0:T(8,128)S(1)} %fusion.15, f32[384]{0:T(512)S(1)} %copy-done.4), kind=kOutput, calls=%fused_computation | convolution fusion | flops 2426929152 | bytes 10619904 | tf_op jit(solution)/shard_map/dot_general | solution.py:82
  176.2 0.0 reduce-scatter.2.cloned.1.call-update
  176.2 0.0 all-gather.6.cloned.1.call-start
  176.3 130.4 %reduce-scatter.2.cloned.1.call-done = bf16[2048,48]{0,1:T(8,128)(2,1)} async-done(((bf16[2048,1536]{0,1:T(8,128)(2,1)}), bf16[2048,48]{0,1:T(8,128)(2,1)}) %reduce-scatter.2.cloned.1.call-update) | async-done | bytes 196624 | tf_op jit(solution)/shard_map/reduce_scatter | solution.py:85
  306.7 1.0 fusion.8
  307.6 0.1 broadcast_in_dim.6
  307.8 23.0 %all_to_all.29 = f32[32,1,2048]{2,1,0:T(1,128)S(1)} all-to-all(f32[32,1,2048]{2,1,0:T(1,128)S(1)} %broadcast_in_dim.6), channel_id=1, replica_groups=mesh['dp'=8,'tensor_0'=8,'tensor_1'=2,'tensor_2'=2] {'tensor_0','tensor_..., dimensions={0} | all-to-all | bytes 524288 | tf_op jit(solution)/shard_map/all_to_all | solution.py:13
  330.8 0.2 reduce_sum.73
  331.0 0.6 multiply_reduce_fusion.1
  331.6 1.0 fusion.9
  332.5 8.2 %all-gather = bf16[4096,48]{0,1:T(8,128)(2,1)S(1)} all-gather(bf16[2048,48]{0,1:T(8,128)(2,1)S(1)} %fusion.9), channel_id=2, replica_groups=mesh['dp'=8,'tensor_0'=8,'tensor_1'=2,'tensor_2'=2] {'tensor_1'}, dimensions={0}, use_global_device_ids=true | all-gather | bytes 589824 | tf_op jit(solution)/shard_map/all_gather | solution.py:30
  340.8 0.8 copy.28
  341.5 0.0 all-gather.6.cloned.1.call-update
  341.6 0.0 all-gather.8.cloned.1.call-start
  341.6 41.2 %all-gather.6.cloned.1.call-done = bf16[16,2048,48]{1,2,0:T(8,128)(2,1)} async-done(((bf16[2,2048,48]{1,2,0:T(8,128)(2,1)}), bf16[16,2048,48]{1,2,0:T(8,128)(2,1)}) %all-gather.6.cloned.1.call-update) | async-done | bytes 3145744 | tf_op jit(solution)/shard_map/all_gather | solution.py:30
  382.8 0.0 all-gather.8.cloned.1.call-update
  382.9 1.2 broadcast_in_dim.16
  384.1 4.9 %all-to-all-start.4 = ((f32[8,1,1]{2,1,0:T(1,128)}), f32[8,1,1]{2,1,0:T(1,128)S(1)}, u32[]{:S(2)}, u32[]{:S(2)}) async-start(f32[8,1,1]{2,1,0:T(1,128)} %broadcast_in_dim.16), calls=%async_computation.5 | async-start | bytes 8192 | tf_op jit(solution)/shard_map/all_to_all | solution.py:13
  389.0 17.7 %all-gather.8.cloned.1.call-done = bf16[16,2,2048,48]{2,3,1,0:T(8,128)(2,1)} async-done(((bf16[8,2,2048,48]{2,3,1,0:T(8,128)(2,1)}), bf16[16,2,2048,48]{2,3,1,0:T(8,128)(2,1)}) %all-gather.8.cloned.1.call-update) | async-done | bytes 6291472 | tf_op jit(solution)/shard_map/all_gather | solution.py:30
  406.7 3.5 copy.18
  410.2 0.0 copy-start.2
  410.2 0.1 copy-done.7
  410.4 5.4 %fusion.12 = (f32[384]{0:T(512)S(1)}, bf16[2048,384]{1,0:T(8,128)(2,1)S(1)}, f32[384]{0:T(512)S(1)}) fusion(f32[2048,384]{1,0:T(8,128)S(1)} %copy-done.7, f32[384]{0:T(512)S(1)} %copy-done.4, f32[384]{0:T(512)S(1)} %copy-done.5, bf16[2048,1536]{0,1:T(8,128)(2,1)S(1)} %bitcast.27, bf16[1536,384]{1,0:T(8,128)(2,1)S(1)} %copy-done), kind=kOutput, calls=%fused_computation.27 | convolution fusion | flops 2431646720 | bytes 12195840 | tf_op jit(solution)/shard_map/dot_general | solution.py:95
  415.8 4.9 %fusion.4 = f32[1536,384]{1,0:T(8,128)} fusion(bf16[2048,1536]{1,0:T(8,128)(2,1)S(1)} %bitcast.26, bf16[2048,384]{1,0:T(8,128)(2,1)S(1)} %get-tuple-element.5), kind=kOutput, calls=%fused_computation.11 | convolution fusion | flops 2415919104 | bytes 10223616 | tf_op jit(solution)/shard_map/dot_general | solution.py:63
  420.7 0.0 all-to-all-done.4
  420.8 0.6 broadcast_in_dim.7
  421.4 4.6 all-to-all-start.3
  426.0 9.4 %convolution_add_fusion = f32[1536,384]{1,0:T(8,128)} fusion(f32[1536,384]{1,0:T(8,128)} %fusion.4, bf16[2048,1536]{0,1:T(8,128)(2,1)} %bitcast.28, f32[384]{0:T(512)S(1)} %copy-done.5, f32[2048,384]{1,0:T(8,128)} %copy-done.6, f32[384]{0:T(512)S(1)} %copy-done.4), kind=kOutput, calls=%fused_computation.10 | convolution fusion | flops 2424373248 | bytes 14158848 | tf_op jit(solution)/shard_map/dot_general | solution.py:63
  435.4 0.0 all-to-all-done.3
  435.4 0.6 copy-done.3
  436.0 5.2 %all-to-all-start.2 = ((f32[8,192,384]{2,1,0:T(8,128)}), f32[8,192,384]{2,1,0:T(8,128)S(1)}, u32[]{:S(2)}, u32[]{:S(2)}) async-start(f32[8,192,384]{2,1,0:T(8,128)} %bitcast.31), calls=%async_computation.3 | async-start | bytes 4718592 | tf_op jit(solution)/shard_map/all_to_all | solution.py:49
  441.2 0.6 reduce_sum.79
  442.4 0.8 reduce_sum.77
  443.2 0.6 fusion.14
  443.8 31.6 %all-to-all-done.2 = f32[8,192,384]{2,1,0:T(8,128)S(1)} async-done(((f32[8,192,384]{2,1,0:T(8,128)}), f32[8,192,384]{2,1,0:T(8,128)S(1)}, u32[]{:S(2)}, u32[]{:S(2)}) %all-to-all-start.2) | async-done | bytes 2359328 | tf_op jit(solution)/shard_map/all_to_all | solution.py:49
  475.4 0.8 reduce_sum.74
  (13 shorter events, 0.0 us)
Async XLA Ops:
  7.2 158.3 %copy-start = (bf16[1536,384]{1,0:T(8,128)(2,1)S(1)}, bf16[1536,384]{1,0:T(8,128)(2,1)}, u32[]{:S(2)}) copy-start(bf16[1536,384]{1,0:T(8,128)(2,1)} %param.9) | copy-start | bytes 3538948
  7.2 299.5 %reduce-scatter.2.cloned.1.call-start = ((), (), s32[]{:S(2)}) async-start(), calls=%async_computation.6 | async-start | bytes 6488064 | tf_op jit(solution)/shard_map/reduce_scatter | solution.py:85
  162.8 2.6 copy-start.1
  165.4 5.1 %copy-start.4 = (f32[384]{0:T(512)S(1)}, f32[384]{0:T(512)}, u32[]{:S(2)}) copy-start(f32[384]{0:T(512)} %param.10) | copy-start | bytes 4612
  165.4 5.1 %copy-start.5 = (f32[384]{0:T(512)S(1)}, f32[384]{0:T(512)}, u32[]{:S(2)}) copy-start(f32[384]{0:T(512)} %param.11) | copy-start | bytes 4612
  168.9 1.6 copy-start.6
  176.2 206.6 %all-gather.6.cloned.1.call-start = ((), (), s32[]{:S(2)}) async-start(), calls=%async_computation.7 | async-start | bytes 3538944 | tf_op jit(solution)/shard_map/all_gather | solution.py:30
  341.6 65.1 %all-gather.8.cloned.1.call-start = ((), (), s32[]{:S(2)}) async-start(), calls=%async_computation.8 | async-start | bytes 9437184 | tf_op jit(solution)/shard_map/all_gather | solution.py:30
  384.1 36.6 %all-to-all-start.4 = ((f32[8,1,1]{2,1,0:T(1,128)}), f32[8,1,1]{2,1,0:T(1,128)S(1)}, u32[]{:S(2)}, u32[]{:S(2)}) async-start(f32[8,1,1]{2,1,0:T(1,128)} %broadcast_in_dim.16), calls=%async_computation.5 | async-start | bytes 8192 | tf_op jit(solution)/shard_map/all_to_all | solution.py:13
  406.7 3.7 copy-start.7
  406.7 9.1 %slice-start = ((s8[6291456]{0:T(1024)(128)(4,1)}), s8[2097152]{0:T(1024)(128)(4,1)S(1)}, s32[]{:S(2)}) async-start(s8[6291456]{0:T(1024)(128)(4,1)} %bitcast.24), calls=%async_computation.9 | async-start | bytes 4194304
  410.2 5.6 %copy-start.2 = (bf16[8,2,2,2048,48]{3,4,2,1,0:T(8,128)(2,1)}, bf16[8,2,2,2048,48]{3,4,2,1,0:T(8,128)(2,1)S(1)}, u32[]{:S(2)}) copy-start(bf16[8,2,2,2048,48]{3,4,2,1,0:T(8,128)(2,1)S(1)} %copy.18) | copy-start | bytes 18874372
  410.4 5.4 %slice-start.1 = ((s8[6291456]{0:T(1024)(128)(4,1)}), s8[4194304]{0:T(1024)(128)(4,1)S(1)}, s32[]{:S(2)}) async-start(s8[6291456]{0:T(1024)(128)(4,1)} %bitcast.24), calls=%async_computation.10 | async-start | bytes 8388608
  421.4 14.0 %all-to-all-start.3 = ((f32[8,1,768]{2,1,0:T(1,128)}), f32[8,1,768]{2,1,0:T(1,128)S(1)}, u32[]{:S(2)}, u32[]{:S(2)}) async-start(f32[8,1,768]{2,1,0:T(1,128)} %broadcast_in_dim.7), calls=%async_computation.4 | async-start | bytes 49152 | tf_op jit(solution)/shard_map/all_to_all | solution.py:13
  435.4 0.6 copy-start.3
  436.0 39.4 %all-to-all-start.2 = ((f32[8,192,384]{2,1,0:T(8,128)}), f32[8,192,384]{2,1,0:T(8,128)S(1)}, u32[]{:S(2)}, u32[]{:S(2)}) async-start(f32[8,192,384]{2,1,0:T(8,128)} %bitcast.31), calls=%async_computation.3 | async-start | bytes 4718592 | tf_op jit(solution)/shard_map/all_to_all | solution.py:49
Sparse Core Ops, SparseCore 0:
  176.3 130.2 reduce-scatter.1
  341.7 41.1 all-gather.5
  384.6 21.9 all-gather.7
